TPU v7x, 256 devices: a whole 4x4x8 slice. The times are simulated.
256 devices in a mesh: dom: 64 (over x, z, y_lo), feat: 4 (over y_hi, core).
Axes of the slice: x: 4, y: 4 (y_hi: 2, y_lo: 2; y = y_hi * 2 + y_lo), z: 8, core: 2. Of those that a mesh axis runs over, the one named last changes fastest.
Arguments:
- embed: bfloat16 [256, 65536], P('feat', 'dom'), may hold values from -6 to 6
- weight: bfloat16 [256, 256], P('feat'), may hold values from -0.375 to 0.375
- cotangent: bfloat16 [256, 65536], P('feat', 'dom'), may hold values from -6 to 6
- edge_masks: int32 [6144, 128, 128], P('dom'), may hold values 0 or 1
- tile_rows: int32 [6144], P('dom'), may hold values from 0 to 7
- tile_owner: int32 [6144, 1], P('dom'), may hold values from 0 to 63; in each aligned block of 96 rows (0 to 95, 96 to 191, ...) at most 2 rows name the same one
- tile_sub: int32 [6144], P('dom'), may hold values from 0 to 7
Outputs:
- output: bfloat16 [256, 65536], P('feat', 'dom')
- embed_grad: float32 [256, 65536], P('feat', 'dom')
- weight_grad: float32 [256, 256], P('feat')
Inputs may be any that keep to these rules, and one draw needn't show every extreme that they name: `tile_owner`: among the 96 tiles of one index of dom no owner is named more than 2 times, a bound that some block reaches.
All inputs are finite; a program needn't handle non-finite values. No bound on the sum of `edge_masks` on one device may be relied on, other than what follows from the above.
Results may differ from a plain program's by a relative error of at most 0.0059.
Values may be sent and summed in bfloat16 or wider, within the bound.
No kernel may reach another device: no remote copies, remote signals or barrier semaphores. Data moves between devices by JAX's collectives and lax.ppermute only.
A program may use at most 64 MiB of HBM per device.

v0:
```python
import math
import jax
import jax.numpy as jnp
from jax import lax
from jax.sharding import PartitionSpec as P


def per_device(embed, weight, cotangent, edge_masks, tile_rows, tile_owner, tile_sub):
    feat_width = embed.shape[0]
    local_nodes = embed.shape[1]
    block_len = edge_masks.shape[1]
    local_blocks = local_nodes // block_len
    dom_count = lax.axis_size("dom")
    nodes_all = local_nodes * dom_count
    block_range = jnp.arange(local_blocks, dtype=jnp.int32)
    col_ids = tile_owner[:, 0] * local_blocks + tile_sub
    own_bf = embed.reshape(feat_width, local_blocks, block_len)
    gathered = lax.all_gather(embed, "dom", axis=1, tiled=True)
    all_blocks = gathered.reshape(feat_width, dom_count * local_blocks, block_len)
    fetched = jnp.take(all_blocks, col_ids, axis=1)
    mask_bf = edge_masks.astype(jnp.bfloat16)
    contrib = jnp.einsum("ftj,tij->fti", fetched, mask_bf, preferred_element_type=jnp.float32)
    row_onehot = (tile_rows[:, None] == block_range[None, :]).astype(jnp.float32)
    neighbour = jnp.einsum("fti,tr->fri", contrib, row_onehot, precision=lax.Precision.HIGHEST)
    row_int = (tile_rows[:, None] == block_range[None, :]).astype(jnp.int32)
    counts = jnp.sum(edge_masks, axis=2)
    degree = jnp.dot(row_int.T, counts)
    inv_root = 1.0 / jnp.sqrt(1.0 + degree.astype(jnp.float32))
    own_blocks = own_bf.astype(jnp.float32)
    aggregate = (
        (own_blocks + neighbour * inv_root[None])
        .astype(jnp.bfloat16)
        .reshape(feat_width, local_nodes)
    )
    pre_act = lax.psum_scatter(
        jnp.einsum("fh,fn->hn", weight, aggregate, preferred_element_type=jnp.float32),
        "feat",
        scatter_dimension=0,
        tiled=True,
    )
    gate_vals = jax.nn.sigmoid(pre_act)
    output = (pre_act * gate_vals).astype(jnp.bfloat16)
    grad_pre = (
        cotangent.astype(jnp.float32) * gate_vals * (1.0 + pre_act * (1.0 - gate_vals))
    ).astype(jnp.bfloat16)
    grad_full = lax.all_gather(grad_pre, "feat", axis=0, tiled=True)
    grad_agg = jnp.einsum("fh,hn->fn", weight, grad_full, preferred_element_type=jnp.float32)
    weight_terms = jnp.einsum("fn,hn->fh", aggregate, grad_full, preferred_element_type=jnp.float32)
    grad_blocks = grad_agg.reshape(feat_width, local_blocks, block_len)
    scaled_grad = (grad_blocks * inv_root[None]).astype(jnp.bfloat16)
    selected = jnp.take(scaled_grad, tile_rows, axis=1)
    partials = jnp.einsum("fti,tij->tfj", selected, mask_bf, preferred_element_type=jnp.float32)
    start = jnp.int32(0)
    inside = (col_ids >= start) & (col_ids < start + lax.axis_size("dom") * local_blocks)
    target = jnp.where(inside, col_ids, lax.axis_size("dom") * local_blocks)
    empty = jnp.zeros((lax.axis_size("dom") * local_blocks, feat_width, block_len), jnp.float32)
    received = lax.psum_scatter(
        empty.at[target].add(partials, mode="drop"), "dom", scatter_dimension=0, tiled=True
    )
    incoming = jnp.transpose(received, (1, 0, 2))
    embed_grad = (grad_blocks + incoming).reshape(feat_width, local_nodes)
    weight_grad = lax.psum(weight_terms, "dom") / math.sqrt(nodes_all)
    return (output, embed_grad, weight_grad)


def solution(mesh):
    in_specs = (
        P("feat", "dom"),
        P("feat", None),
        P("feat", "dom"),
        P("dom", None, None),
        P("dom"),
        P("dom", None),
        P("dom"),
    )
    out_specs = (P("feat", "dom"), P("feat", "dom"), P("feat", None))
    return jax.shard_map(
        per_device, mesh=mesh, in_specs=in_specs, out_specs=out_specs, check_vma=False
    )
```

profile of v0, /device:TPU:16, one launch (start us, length us, event | category | flops | bytes accessed | tf_op | source)
XLA Modules:
  0.0 1295.9 jit_solution(5123875509077076049)
XLA Ops:
  7.2 0.0 copy-start
  7.2 0.0 all-gather.2.cloned.1.call-start
  7.2 0.7 all-gather.2.cloned.1.call-update
  7.9 0.0 reduce-scatter.7.cloned.1.call-start
  8.0 0.9 convert_bitcast_fusion
  8.9 0.0 copy-start.3
  9.0 0.0 copy-start.4
  9.0 0.0 copy-start.2
  9.0 4.5 reduce_sum.9
  13.5 0.0 copy-done.3
  13.5 0.0 copy-done.4
  13.5 0.0 copy-done.2
  13.5 0.1 fusion.24
  13.7 312.7 %all-gather.2.cloned.1.call-done = bf16[64,65536]{1,0:T(8,128)(2,1)} async-done(((bf16[64,1024]{1,0:T(8,128)(2,1)}), bf16[64,65536]{1,0:T(8,128)(2,1)}) %all-gather.2.cloned.1.call-update) | async-done | bytes 8388624 | tf_op jit(solution)/shard_map/all_gather | solution.py:18
  326.3 9.0 copy_bitcast_fusion
  335.4 4.2 gather_fusion
  339.6 5.0 convolution_bitcast_fusion
  344.6 0.0 copy-start.1
  344.6 2.9 fusion.20
  347.5 0.0 copy-done
  347.5 0.3 convolution_bitcast_fusion.1
  347.9 1.3 copy.39
  349.2 0.0 reduce-scatter.7.cloned.1.call-update
  349.2 0.0 all-reduce.2.cloned.1.call-start
  349.3 31.4 %reduce-scatter.7.cloned.1.call-done = f32[64,1024]{1,0:T(8,128)} async-done(((f32[256,1024]{1,0:T(8,128)}), f32[64,1024]{1,0:T(8,128)}) %reduce-scatter.7.cloned.1.call-update) | async-done | bytes 262160 | tf_op jit(solution)/shard_map/reduce_scatter | solution.py:35
  380.7 0.0 copy-done.1
  380.7 1.7 multiply_convert_fusion
  382.4 8.9 all_gather.7
  391.4 0.9 fusion.29
  392.3 0.2 convolution_bitcast_fusion.2
  392.5 0.0 all-reduce.2.cloned.1.call-update
  392.5 0.2 reduce-scatter.5.cloned.1.call-start
  392.8 2.0 gather_fusion.1
  394.7 4.3 fusion.2
  399.0 7.9 broadcast_in_dim.39
  406.9 13.4 %scatter_fusion = f32[512,64,128]{2,1,0:T(8,128)} fusion(f32[512,64,128]{2,1,0:T(8,128)} %broadcast_in_dim.39, s32[96]{0:T(128)S(1)} %compare_select_fusion.1, f32[96,64,128]{2,1,0:T(8,128)S(1)} %fusion.2), kind=kCustom, calls=%fused_computation.2 | custom fusion | flops 786432 | bytes 9437568 | tf_op jit(solution)/shard_map/scatter-add | solution.py:58
  420.3 0.0 reduce-scatter.5.cloned.1.call-update
  420.4 498.3 %all-reduce.2.cloned.1.call-done = f32[64,256]{1,0:T(8,128)} async-done(((f32[64,256]{1,0:T(8,128)}), f32[64,256]{1,0:T(8,128)}) %all-reduce.2.cloned.1.call-update) | async-done | bytes 65552 | tf_op jit(solution)/shard_map/psum | solution.py:62
  918.6 1.5 broadcast_multiply_fusion
  920.1 367.6 %reduce-scatter.5.cloned.1.call-done = f32[8,64,128]{2,1,0:T(8,128)} async-done(((f32[512,64,128]{2,1,0:T(8,128)}), f32[8,64,128]{2,1,0:T(8,128)}) %reduce-scatter.5.cloned.1.call-update) | async-done | bytes 262160 | tf_op jit(solution)/shard_map/reduce_scatter | solution.py:57
  1287.7 1.7 copy_bitcast_fusion.1
  (8 shorter events, 0.1 us)
Async XLA Ops:
  7.2 340.3 %copy-start = (bf16[64,256]{1,0:T(8,128)(2,1)S(1)}, bf16[64,256]{1,0:T(8,128)(2,1)}, u32[]{:S(2)}) copy-start(bf16[64,256]{1,0:T(8,128)(2,1)} %param.8) | copy-start | bytes 98308
  7.2 319.2 %all-gather.2.cloned.1.call-start = ((), (), s32[]{:S(2)}) async-start(), calls=%async_computation.2 | async-start | bytes 8519680 | tf_op jit(solution)/shard_map/all_gather | solution.py:18
  7.9 372.8 %reduce-scatter.7.cloned.1.call-start = ((), (), s32[]{:S(2)}) async-start(), calls=%async_computation.5 | async-start | bytes 1310720 | tf_op jit(solution)/shard_map/reduce_scatter | solution.py:35
  8.9 4.5 copy-start.3
  9.0 4.5 copy-start.4
  9.0 4.6 copy-start.2
  344.6 36.1 %copy-start.1 = (bf16[64,1024]{1,0:T(8,128)(2,1)S(1)}, bf16[64,1024]{1,0:T(8,128)(2,1)}, u32[]{:S(2)}) copy-start(bf16[64,1024]{1,0:T(8,128)(2,1)} %param.9) | copy-start | bytes 393220
  349.2 569.5 %all-reduce.2.cloned.1.call-start = ((), (), s32[]{:S(2)}) async-start(), calls=%async_computation.4 | async-start | bytes 131072 | tf_op jit(solution)/shard_map/psum | solution.py:62
  392.5 895.2 %reduce-scatter.5.cloned.1.call-start = ((), (), s32[]{:S(2)}) async-start(), calls=%async_computation.3 | async-start | bytes 17039360 | tf_op jit(solution)/shard_map/reduce_scatter | solution.py:57
Sparse Core Ops, SparseCore 0:
  9.8 316.4 all-gather.1
  349.3 31.3 reduce-scatter.6
  392.6 525.9 all-reduce.1
  921.1 366.5 reduce-scatter.4
where the time goes:
time: 1300 us
  waiting for transfers between devices  1210 us (93%)
  local copies, waits for them, and re-layouts  24.5 us (2%)
  other arithmetic  23.8 us (2%)
  between operations  13.9 us (1%)
  matrix products  13.8 us (1%)
    psum x1, waiting for transfers between devices, per_device(): weight_grad = lax.psum(weight_terms, 'dom') / math.sqrt(nodes_all)  498 us
    reduce_scatter x1, waiting for transfers between devices, per_device(): lax.psum_scatter(empty.at[target].add(partials, mode='drop'), 'dom', scat...  368 us
    all_gather x1, waiting for transfers between devices, per_device(): gathered = lax.all_gather(embed, 'dom', axis=1, tiled=True)  313 us
    reduce_scatter x1, waiting for transfers between devices, per_device(): lax.psum_scatter(jnp.einsum('fh,fn->hn', weight, aggregate, preferred_ele...  31.4 us
  transfers between devices with their start and end apart: 4, of which 4 were waited for; matrix products, arithmetic and copies ran while one was open for 3% of the time, Pallas kernels for 0%

commit v1 on v0

--- a/solution.py
+++ b/solution.py
@@ -15,7 +15,9 @@
     block_range = jnp.arange(local_blocks, dtype=jnp.int32)
     col_ids = tile_owner[:, 0] * local_blocks + tile_sub
     own_bf = embed.reshape(feat_width, local_blocks, block_len)
-    gathered = lax.all_gather(embed, "dom", axis=1, tiled=True)
+    gathered = jnp.concatenate(
+        lax.all_to_all(jnp.stack(lax.axis_size("dom") * [embed], axis=0), "dom", 0, 0), 1
+    )
     all_blocks = gathered.reshape(feat_width, dom_count * local_blocks, block_len)
     fetched = jnp.take(all_blocks, col_ids, axis=1)
     mask_bf = edge_masks.astype(jnp.bfloat16)

time: 1300 us -> 1210 us (0.931)
  waiting for transfers between devices: 1210 us -> 1080 us
  local copies, waits for them, and re-layouts: 24.5 us -> 57.3 us
  starting transfers between devices: 0.34 us -> 13.4 us
    all_gather x1 -> x0, waiting for transfers between devices: 313 us -> none  [per_device(): gathered = lax.all_gather(embed, 'dom', axis=1, tiled=True)]
    all_to_all x0 -> x1, waiting for transfers between devices: none -> 183 us  [per_device(): lax.all_to_all(jnp.stack(lax.axis_size('dom') * [embed], axis=0), 'dom',...]
    another operation x0 -> x3, local copies, waits for them, and re-layouts: none -> 30.5 us  [the longest x2 25.3 us: per_device(): gathered.reshape(feat_width, dom_count * local_blocks, block_len)]
    all_to_all x0 -> x1, starting transfers between devices: none -> 13 us  [per_device(): lax.all_to_all(jnp.stack(lax.axis_size('dom') * [embed], axis=0), 'dom',...]
where the time goes in v1:
time: 1210 us
  waiting for transfers between devices  1080 us (89%)
  local copies, waits for them, and re-layouts  57.3 us (5%)
  other arithmetic  22.9 us (2%)
  between operations  13.9 us (1%)
  matrix products  13.8 us (1%)
  starting transfers between devices  13.4 us (1%)
    psum x1, waiting for transfers between devices, per_device(): weight_grad = lax.psum(weight_terms, 'dom') / math.sqrt(nodes_all)  499 us
    reduce_scatter x1, waiting for transfers between devices, per_device(): lax.psum_scatter(empty.at[target].add(partials, mode='drop'), 'dom', scat...  368 us
    all_to_all x1, waiting for transfers between devices, per_device(): lax.all_to_all(jnp.stack(lax.axis_size('dom') * [embed], axis=0), 'dom',...  183 us
    reduce_scatter x1, waiting for transfers between devices, per_device(): lax.psum_scatter(jnp.einsum('fh,fn->hn', weight, aggregate, preferred_ele...  33.1 us
    another operation x2, local copies, waits for them, and re-layouts, per_device(): gathered.reshape(feat_width, dom_count * local_blocks, block_len)  25.3 us
  transfers between devices with their start and end apart: 4, of which 4 were waited for; matrix products, arithmetic and copies ran while one was open for 3% of the time, Pallas kernels for 0%

profile of v1, /device:TPU:16, one launch (start us, length us, event | category | flops | bytes accessed | tf_op | source)
XLA Modules:
  0.0 1212.7 jit_solution(490654940084653423)
XLA Ops:
  7.2 0.0 copy-start
  7.2 5.2 stack.2
  12.4 0.0 copy-start.1
  12.4 13.0 %all-to-all-start = ((bf16[64,64,1024]{2,1,0:T(8,128)(2,1)}), bf16[64,64,1024]{2,1,0:T(8,128)(2,1)}, u32[]{:S(2)}, u32[]{:S(2)}) async-start(bf16[64,64,1024]{2,1,0:T(8,128)(2,1)} %stack.2), calls=%async_computation | async-start | bytes 16777216 | tf_op jit(solution)/shard_map/all_to_all | solution.py:19
  25.4 0.0 reduce-scatter.7.cloned.1.call-start
  25.5 0.0 copy-done.1
  25.6 0.0 copy-start.4
  25.6 0.0 copy-start.5
  25.6 0.0 copy-start.3
  25.6 4.5 reduce_sum.9
  30.1 0.0 copy-done.4
  30.1 0.0 copy-done.5
  30.2 0.0 copy-done.3
  30.2 0.1 fusion.24
  30.3 182.6 %all-to-all-done = bf16[64,64,1024]{2,1,0:T(8,128)(2,1)} async-done(((bf16[64,64,1024]{2,1,0:T(8,128)(2,1)}), bf16[64,64,1024]{2,1,0:T(8,128)(2,1)}, u32[]{:S(2)}, u32[]{:S(2)}) %all-to-all-start) | async-done | bytes 8388640 | tf_op jit(solution)/shard_map/all_to_all | solution.py:19
  212.9 11.3 copy.33
  224.2 13.3 %reshape_reshape.3 = bf16[64,512,128]{2,1,0:T(8,128)(2,1)} reshape(bf16[64,64,1024]{2,1,0:T(8,128)(2,1)} %copy.33) | data formatting | bytes 16777216 | tf_op jit(solution)/shard_map/reshape;reshape | solution.py:21
  237.5 12.0 copy.34
  249.5 4.2 gather_fusion
  253.8 5.0 convolution_bitcast_fusion
  258.8 0.0 copy-start.2
  258.8 2.9 fusion.20
  261.7 0.0 copy-done
  261.7 0.3 convolution_bitcast_fusion.1
  262.0 1.3 copy.42
  263.3 0.0 reduce-scatter.7.cloned.1.call-update
  263.3 0.0 all-reduce.2.cloned.1.call-start
  263.4 33.1 %reduce-scatter.7.cloned.1.call-done = f32[64,1024]{1,0:T(8,128)} async-done(((f32[256,1024]{1,0:T(8,128)}), f32[64,1024]{1,0:T(8,128)}) %reduce-scatter.7.cloned.1.call-update) | async-done | bytes 262160 | tf_op jit(solution)/shard_map/reduce_scatter | solution.py:37
  296.5 0.0 copy-done.2
  296.5 1.7 multiply_convert_fusion
  298.3 8.9 all_gather.3
  307.2 0.9 fusion.29
  308.1 0.2 convolution_bitcast_fusion.2
  308.3 0.0 all-reduce.2.cloned.1.call-update
  308.3 0.3 reduce-scatter.5.cloned.1.call-start
  308.6 2.0 gather_fusion.1
  310.6 4.3 fusion.2
  314.9 7.9 broadcast_in_dim.39
  322.7 13.4 %scatter_fusion = f32[512,64,128]{2,1,0:T(8,128)} fusion(f32[512,64,128]{2,1,0:T(8,128)} %broadcast_in_dim.39, s32[96]{0:T(128)S(1)} %compare_select_fusion.1, f32[96,64,128]{2,1,0:T(8,128)S(1)} %fusion.2), kind=kCustom, calls=%fused_computation.2 | custom fusion | flops 786432 | bytes 9437568 | tf_op jit(solution)/shard_map/scatter-add | solution.py:60
  336.2 0.0 reduce-scatter.5.cloned.1.call-update
  336.2 499.0 %all-reduce.2.cloned.1.call-done = f32[64,256]{1,0:T(8,128)} async-done(((f32[64,256]{1,0:T(8,128)}), f32[64,256]{1,0:T(8,128)}) %all-reduce.2.cloned.1.call-update) | async-done | bytes 65552 | tf_op jit(solution)/shard_map/psum | solution.py:64
  835.2 1.5 broadcast_multiply_fusion
  836.7 367.7 %reduce-scatter.5.cloned.1.call-done = f32[8,64,128]{2,1,0:T(8,128)} async-done(((f32[512,64,128]{2,1,0:T(8,128)}), f32[8,64,128]{2,1,0:T(8,128)}) %reduce-scatter.5.cloned.1.call-update) | async-done | bytes 262160 | tf_op jit(solution)/shard_map/reduce_scatter | solution.py:59
  1204.5 1.7 copy_bitcast_fusion
  (9 shorter events, 0.1 us)
Async XLA Ops:
  7.2 254.5 %copy-start = (bf16[64,256]{1,0:T(8,128)(2,1)S(1)}, bf16[64,256]{1,0:T(8,128)(2,1)}, u32[]{:S(2)}) copy-start(bf16[64,256]{1,0:T(8,128)(2,1)} %param.8) | copy-start | bytes 98308
  12.4 13.1 %copy-start.1 = (bf16[64,1024]{1,0:T(8,128)(2,1)S(1)}, bf16[64,1024]{1,0:T(8,128)(2,1)}, u32[]{:S(2)}) copy-start(bf16[64,1024]{1,0:T(8,128)(2,1)} %param.7) | copy-start | bytes 393220
  12.4 200.5 %all-to-all-start = ((bf16[64,64,1024]{2,1,0:T(8,128)(2,1)}), bf16[64,64,1024]{2,1,0:T(8,128)(2,1)}, u32[]{:S(2)}, u32[]{:S(2)}) async-start(bf16[64,64,1024]{2,1,0:T(8,128)(2,1)} %stack.2), calls=%async_computation | async-start | bytes 16777216 | tf_op jit(solution)/shard_map/all_to_all | solution.py:19
  25.4 271.1 %reduce-scatter.7.cloned.1.call-start = ((), (), s32[]{:S(2)}) async-start(), calls=%async_computation.5 | async-start | bytes 1310720 | tf_op jit(solution)/shard_map/reduce_scatter | solution.py:37
  25.6 4.5 copy-start.4
  25.6 4.5 copy-start.5
  25.6 4.6 copy-start.3
  258.8 37.8 %copy-start.2 = (bf16[64,1024]{1,0:T(8,128)(2,1)S(1)}, bf16[64,1024]{1,0:T(8,128)(2,1)}, u32[]{:S(2)}) copy-start(bf16[64,1024]{1,0:T(8,128)(2,1)} %param.9) | copy-start | bytes 393220
  263.3 571.9 %all-reduce.2.cloned.1.call-start = ((), (), s32[]{:S(2)}) async-start(), calls=%async_computation.4 | async-start | bytes 131072 | tf_op jit(solution)/shard_map/psum | solution.py:64
  308.3 896.1 %reduce-scatter.5.cloned.1.call-start = ((), (), s32[]{:S(2)}) async-start(), calls=%async_computation.3 | async-start | bytes 17039360 | tf_op jit(solution)/shard_map/reduce_scatter | solution.py:59
Sparse Core Ops, SparseCore 0:
  263.5 33.0 reduce-scatter.6
  308.4 526.7 all-reduce.1
  837.8 366.6 reduce-scatter.4
